TPU v7x, 512 devices: a whole 4x8x8 slice. The times are simulated.
512 devices in a mesh: span: 4 (over x), seq: 32 (over z_hi, y, core), head: 4 (over z_lo).
Axes of the slice: x: 4, y: 8, z: 8 (z_hi: 2, z_lo: 4; z = z_hi * 4 + z_lo), core: 2. Of those that a mesh axis runs over, the one named last changes fastest.
Arguments:
- query_proj: bfloat16 [4, 1280, 3072], P('span', 'seq', 'head'), may hold values from -12 to 12
- key_proj: bfloat16 [4, 1280, 3072], P('span', 'seq', 'head'), may hold values from -12 to 12
- value_proj: bfloat16 [4, 1280, 3072], P('span', 'seq', 'head'), may hold values from -24 to 24
- block_order: int32 [4], replicated, may hold values from 0 to 3, each once
- valid_frames: int32 [4], replicated, may hold values from 1 to 8, as said below
- noise_steps: int32 [4], replicated, may hold values from 0 to 3
- gate_table: float32 [4, 6144], P(None, 'seq'), may hold values from 1 to 10
- out_weight: bfloat16 [3072, 6144], P('head', 'seq'), may hold values from -0.109375 to 0.109375
- residual: bfloat16 [4, 1280, 6144], P('span', 'head', 'seq'), may hold values from -3 to 3
Outputs:
- mixed: bfloat16 [4, 1280, 6144], P('span', 'head', 'seq')
Inputs may be any that keep to these rules, and one draw needn't show every extreme that they name: `valid_frames`: some block has all 8 frames open.
All inputs are finite; a program needn't handle non-finite values.
Results may differ from a plain program's by a relative error of at most 0.017.
Values may be sent and summed in bfloat16 or wider, within the bound.
No kernel may reach another device: no remote copies, remote signals or barrier semaphores. Data moves between devices by JAX's collectives and lax.ppermute only.
A program may use at most 128 MiB of HBM per device.

v0:
```python
import jax
import jax.numpy as jnp
from jax import lax
from jax.sharding import PartitionSpec as P

HD = 128
FRAMES = 8
floor_score = -1e30


def lookup(entries, picked):
    slots = jnp.arange(entries.shape[0], dtype=jnp.int32)
    return jnp.sum(jnp.where(slots[None, :] == picked[:, None], entries[None, :], 0), axis=1)


def attend(carry_state, queries, keys_piece, values_piece, visible):
    running_max, denominator, summed = carry_state
    score_scale = 1.0 / queries.shape[-1] ** 0.5
    scores = (
        jnp.einsum("qhe,khe->hqk", queries, keys_piece, preferred_element_type=jnp.float32)
        * score_scale
    )
    scores = jnp.where(visible[None, None, :], scores, floor_score)
    new_max = jnp.maximum(running_max, jnp.max(scores, axis=2))
    weights = jnp.where(visible[None, None, :], jnp.exp(scores - new_max[:, :, None]), 0.0)
    denominator = jnp.sum(weights, axis=2)
    summed = jnp.einsum(
        "hqk,khe->hqe",
        weights.astype(jnp.bfloat16),
        values_piece,
        preferred_element_type=jnp.float32,
    )
    return (new_max, denominator, summed)


def attend_some(carry_state, queries, keys_piece, values_piece, visible):
    return attend(carry_state, queries, keys_piece, values_piece, visible)


def shards(
    query_proj,
    key_proj,
    value_proj,
    block_order,
    valid_frames,
    noise_steps,
    gate_table,
    out_weight,
    residual,
):
    head_dim = HD
    tokens_here = query_proj.shape[1]
    block_len = tokens_here * lax.axis_size("seq")
    frame_len = block_len // FRAMES
    heads_here = query_proj.shape[2] // head_dim
    block_here = lax.axis_index("span")
    order_here = lookup(block_order, jnp.full((1,), block_here, jnp.int32))[0]
    queries = query_proj[0].reshape(tokens_here, heads_here, head_dim)
    start_state = (
        jnp.full((heads_here, tokens_here), floor_score, jnp.float32),
        jnp.zeros((heads_here, tokens_here), jnp.float32),
        jnp.zeros((heads_here, tokens_here, head_dim), jnp.float32),
    )
    keys_piece = lax.all_gather(key_proj, ("span", "seq"), axis=1, tiled=True)
    values_piece = lax.all_gather(value_proj, ("span", "seq"), axis=1, tiled=True)
    count_rows = keys_piece.shape[1]
    positions = jnp.arange(count_rows, dtype=jnp.int32)
    owners = positions // block_len
    frame_index = positions % block_len // frame_len
    visible = (lookup(block_order, owners) <= order_here) & (
        frame_index < lookup(valid_frames, owners)
    )
    final_state = attend_some(
        start_state,
        queries,
        keys_piece[0].reshape(count_rows, heads_here, head_dim),
        values_piece[0].reshape(count_rows, heads_here, head_dim),
        visible,
    )
    running_max, denominator, summed = final_state
    attended = (
        (summed / denominator[:, :, None])
        .transpose(1, 0, 2)
        .reshape(tokens_here, heads_here * head_dim)
        .astype(jnp.bfloat16)
    )
    partial_sums = jnp.dot(
        lax.all_gather(attended, "seq", axis=0, tiled=True),
        out_weight,
        preferred_element_type=jnp.float32,
    )
    head_total = lax.psum_scatter(
        partial_sums.astype(jnp.bfloat16), "head", scatter_dimension=0, tiled=True
    ).astype(jnp.float32)
    step_here = lookup(noise_steps, jnp.full((1,), block_here, jnp.int32))[0]
    step_slots = jnp.arange(gate_table.shape[0], dtype=jnp.int32)
    gate_row = jnp.sum(jnp.where((step_slots == step_here)[:, None], gate_table, 0.0), axis=0)
    mixed = (residual[0].astype(jnp.float32) + gate_row[None, :] * head_total).astype(jnp.bfloat16)
    return mixed[None]


def solution(mesh):
    placed = (
        P("span", "seq", "head"),
        P("span", "seq", "head"),
        P("span", "seq", "head"),
        P(),
        P(),
        P(),
        P(None, "seq"),
        P("head", "seq"),
        P("span", "head", "seq"),
    )
    return jax.shard_map(
        shards, mesh=mesh, in_specs=placed, out_specs=P("span", "head", "seq"), check_vma=False
    )
```

profile of v0, /device:TPU:2, one launch (start us, length us, event | category | flops | bytes accessed | tf_op | source)
XLA Modules:
  0.0 468.5 jit_solution(13273609546740067536)
XLA Ops:
  6.5 0.0 copy-start
  6.5 0.0 all-gather.4.cloned.1.call-start
  6.5 0.7 all-gather.4.cloned.1.call-update
  7.3 0.0 all-gather.6.cloned.1.call-start
  7.3 0.7 all-gather.6.cloned.1.call-update
  8.0 0.0 all-gather.8.cloned.1.call-start
  8.1 0.9 reshape_squeeze.9
  9.0 1.3 fusion.38
  10.3 0.8 select_reduce_fusion
  11.1 0.7 compare_and_fusion
  11.8 161.0 %all-gather.4.cloned.1.call-done = bf16[1,5120,768]{2,1,0:T(8,128)(2,1)} async-done(((bf16[1,40,768]{2,1,0:T(8,128)(2,1)}), bf16[1,5120,768]{2,1,0:T(8,128)(2,1)}) %all-gather.4.cloned.1.call-update) | async-done | bytes 7864336 | tf_op jit(solution)/shard_map/all_gather | solution.py:64
  172.9 10.7 %copy.23 = bf16[1,5120,768]{1,2,0:T(8,128)(2,1)} copy(bf16[1,5120,768]{2,1,0:T(8,128)(2,1)} %all-gather.4.cloned.1.call-done) | data formatting | bytes 15728640 | tf_op jit(solution)/shard_map/all_gather | solution.py:64
  183.6 4.8 %fusion.40 = (f32[6,40]{1,0:T(8,128)S(1)}, f32[6,40,5120]{2,1,0:T(8,128)S(1)}) fusion(bf16[5120,6,128]{0,2,1:T(8,128)(2,1)} %bitcast.27, bf16[40,6,128]{2,1,0:T(8,128)(2,1)S(1)} %reshape_squeeze.9, pred[5120]{0:T(1024)(128)(4,1)S(1)} %compare_and_fusion), kind=kOutput, calls=%fused_computation.50 | convolution fusion | flops 318258944 | bytes 12847040 | tf_op jit(solution)/shard_map/qhe,khe->hqk/dot_general | solution.py:20
  188.4 0.0 copy-start.1
  188.4 2.2 copy-done.1
  190.6 1.1 fusion.1
  191.7 135.4 %all-gather.6.cloned.1.call-done = bf16[1,5120,768]{2,1,0:T(8,128)(2,1)} async-done(((bf16[1,40,768]{2,1,0:T(8,128)(2,1)}), bf16[1,5120,768]{2,1,0:T(8,128)(2,1)}) %all-gather.6.cloned.1.call-update) | async-done | bytes 7864336 | tf_op jit(solution)/shard_map/all_gather | solution.py:65
  327.1 10.4 %copy.26 = bf16[1,5120,768]{1,2,0:T(8,128)(2,1)} copy(bf16[1,5120,768]{2,1,0:T(8,128)(2,1)} %all-gather.6.cloned.1.call-done) | data formatting | bytes 15728640 | tf_op jit(solution)/shard_map/all_gather | solution.py:65
  337.5 0.0 copy-start.4
  337.5 0.0 copy-start.3
  337.5 7.7 %fusion.17 = bf16[6,5,8,128]{3,2,1,0:T(8,128)(2,1)S(1)} fusion(bf16[5120,6,128]{0,2,1:T(8,128)(2,1)} %bitcast.26, f32[6,40,5120]{2,1,0:T(8,128)} %copy-done.1, f32[6,40]{1,0:T(8,128)S(1)} %broadcast_maximum_fusion, pred[5120]{0:T(1024)(128)(4,1)S(1)} %compare_and_fusion, f32[40,6]{0,1:T(8,128)S(1)} %bitcast.29), kind=kOutput, calls=%fused_computation.13 | convolution fusion | flops 318320640 | bytes 12848000 | tf_op jit(solution)/shard_map/hqk,khe->hqe/dot_general | solution.py:27
  345.1 0.0 copy-start.2
  345.2 0.6 copy.39
  345.8 0.0 all-gather.8.cloned.1.call-update
  345.8 0.0 reduce-scatter.4.cloned.1.call-start
  345.9 86.9 %all-gather.8.cloned.1.call-done = bf16[1280,768]{1,0:T(8,128)(2,1)} async-done(((bf16[40,768]{1,0:T(8,128)(2,1)}), bf16[1280,768]{1,0:T(8,128)(2,1)}) %all-gather.8.cloned.1.call-update) | async-done | bytes 1966096 | tf_op jit(solution)/shard_map/all_gather | solution.py:88
  432.7 0.0 copy-done
  432.7 2.3 convolution_convert_fusion
  435.1 1.1 copy.31
  436.1 0.0 reduce-scatter.4.cloned.1.call-update
  436.2 0.0 copy-done.4
  436.2 0.6 fusion.37
  436.8 0.6 iota_compare_fusion.1
  437.5 0.0 copy-done.3
  437.5 0.1 select_reduce_fusion.2
  437.6 22.5 %reduce-scatter.4.cloned.1.call-done = bf16[320,192]{1,0:T(8,128)(2,1)} async-done(((bf16[1280,192]{1,0:T(8,128)(2,1)}), bf16[320,192]{1,0:T(8,128)(2,1)}) %reduce-scatter.4.cloned.1.call-update) | async-done | bytes 122896
  460.1 1.1 copy.32
  461.2 0.0 copy-done.2
  461.2 0.8 fusion.21
  (2 shorter events, 0.0 us)
Async XLA Ops:
  6.5 426.2 %copy-start = (bf16[768,192]{0,1:T(8,128)(2,1)S(1)}, bf16[768,192]{0,1:T(8,128)(2,1)}, u32[]{:S(2)}) copy-start(bf16[768,192]{0,1:T(8,128)(2,1)} %param.16) | copy-start | bytes 884740
  6.5 166.3 %all-gather.4.cloned.1.call-start = ((), (), s32[]{:S(2)}) async-start(), calls=%async_computation.1 | async-start | bytes 7925760 | tf_op jit(solution)/shard_map/all_gather | solution.py:64
  7.3 319.8 %all-gather.6.cloned.1.call-start = ((), (), s32[]{:S(2)}) async-start(), calls=%async_computation.2 | async-start | bytes 7925760 | tf_op jit(solution)/shard_map/all_gather | solution.py:65
  8.0 424.7 %all-gather.8.cloned.1.call-start = ((), (), s32[]{:S(2)}) async-start(), calls=%async_computation.3 | async-start | bytes 2027520 | tf_op jit(solution)/shard_map/all_gather | solution.py:88
  188.4 2.2 copy-start.1
  337.5 98.7 %copy-start.4 = (s32[4]{0:T(128)S(1)}, s32[4]{0:T(128)}, u32[]{:S(2)}) copy-start(s32[4]{0:T(128)} %param.14) | copy-start | bytes 52
  337.5 100.0 %copy-start.3 = (f32[4,192]{1,0:T(4,128)S(1)}, f32[4,192]{1,0:T(4,128)}, u32[]{:S(2)}) copy-start(f32[4,192]{1,0:T(4,128)} %param.15) | copy-start | bytes 9220
  345.1 116.0 %copy-start.2 = (bf16[1,320,192]{1,2,0:T(8,128)(2,1)S(1)}, bf16[1,320,192]{1,2,0:T(8,128)(2,1)}, u32[]{:S(2)}) copy-start(bf16[1,320,192]{1,2,0:T(8,128)(2,1)} %param.17) | copy-start | bytes 368644
  345.8 114.3 %reduce-scatter.4.cloned.1.call-start = ((), (), s32[]{:S(2)}) async-start(), calls=%async_computation.4 | async-start | bytes 819200
Sparse Core Ops, SparseCore 0:
  12.0 160.8 all-gather.3
  177.5 149.5 all-gather.5
  345.9 86.7 all-gather.7
  436.3 23.7 reduce-scatter.3
where the time goes:
time: 469 us; the launch traced here: 468 us
  waiting for transfers between devices  407 us (87%)
  local copies, waits for them, and re-layouts  27 us (6%)
  matrix products  14.8 us (3%)
  between operations  13.2 us (3%)
  other arithmetic  6.04 us (1%)
    all_gather x1, waiting for transfers between devices, shards(): keys_piece = lax.all_gather(key_proj, ('span', 'seq'), axis=1, tiled=True)  161 us
    all_gather x1, waiting for transfers between devices, shards(): lax.all_gather(value_proj, ('span', 'seq'), axis=1, tiled=True)  135 us
    all_gather x1, waiting for transfers between devices, shards(): lax.all_gather(attended, 'seq', axis=0, tiled=True)  86.9 us
    unnamed x5, waiting for transfers between devices  24 us
    all_gather x1, local copies, waits for them, and re-layouts, shards(): keys_piece = lax.all_gather(key_proj, ('span', 'seq'), axis=1, tiled=True)  10.7 us
    all_gather x1, local copies, waits for them, and re-layouts, shards(): lax.all_gather(value_proj, ('span', 'seq'), axis=1, tiled=True)  10.4 us
  transfers between devices with their start and end apart: 4, of which 4 were waited for; matrix products, arithmetic and copies ran while one was open for 5% of the time, Pallas kernels for 0%

commit v1 on v0

--- a/solution.py
+++ b/solution.py
@@ -48,6 +48,12 @@
     out_weight,
     residual,
 ):
+
+    def attach_chains(frame, which_axis):
+        return jnp.concatenate(
+            lax.all_to_all(jnp.stack([frame] * lax.axis_size(which_axis)), which_axis, 0, 0), axis=0
+        )
+
     head_dim = HD
     tokens_here = query_proj.shape[1]
     block_len = tokens_here * lax.axis_size("seq")
@@ -85,9 +91,7 @@
         .astype(jnp.bfloat16)
     )
     partial_sums = jnp.dot(
-        lax.all_gather(attended, "seq", axis=0, tiled=True),
-        out_weight,
-        preferred_element_type=jnp.float32,
+        attach_chains(attended, "seq"), out_weight, preferred_element_type=jnp.float32
     )
     head_total = lax.psum_scatter(
         partial_sums.astype(jnp.bfloat16), "head", scatter_dimension=0, tiled=True

time: 469 us -> 438 us (0.934)
  waiting for transfers between devices: 407 us -> 321 us
  blocking collectives: 0 us -> 56.6 us
    all_gather x1 -> x0, waiting for transfers between devices: 86.9 us -> none  [shards(): lax.all_gather(attended, 'seq', axis=0, tiled=True)]
    all_to_all x0 -> x1, blocking collectives: none -> 56.6 us  [attach_chains(): lax.all_to_all(jnp.stack([frame] * lax.axis_size(which_axis)), which_axis...]
    unnamed x5 -> x4, waiting for transfers between devices: 24 us -> 24.6 us
  transfers between devices with their start and end apart: 4 -> 3, of which waited for: 4 -> 3; matrix products, arithmetic and copies ran while one was open for 5% -> 5% of each run, Pallas kernels for 0% -> 0%
where the time goes in v1:
time: 438 us; the launch traced here: 437 us
  waiting for transfers between devices  321 us (73%)
  blocking collectives  56.6 us (13%)
  local copies, waits for them, and re-layouts  26.5 us (6%)
  matrix products  13.3 us (3%)
  between operations  13.2 us (3%)
  other arithmetic  6.04 us (1%)
    all_gather x1, waiting for transfers between devices, shards(): keys_piece = lax.all_gather(key_proj, ('span', 'seq'), axis=1, tiled=True)  161 us
    all_gather x1, waiting for transfers between devices, shards(): lax.all_gather(value_proj, ('span', 'seq'), axis=1, tiled=True)  135 us
    all_to_all x1, blocking collectives, attach_chains(): lax.all_to_all(jnp.stack([frame] * lax.axis_size(which_axis)), which_axis...  56.6 us
    unnamed x4, waiting for transfers between devices  24.6 us
    all_gather x1, local copies, waits for them, and re-layouts, shards(): keys_piece = lax.all_gather(key_proj, ('span', 'seq'), axis=1, tiled=True)  10.7 us
    all_gather x1, local copies, waits for them, and re-layouts, shards(): lax.all_gather(value_proj, ('span', 'seq'), axis=1, tiled=True)  10.4 us
  transfers between devices with their start and end apart: 3, of which 3 were waited for; matrix products, arithmetic and copies ran while one was open for 5% of the time, Pallas kernels for 0%

profile of v1, /device:TPU:2, one launch (start us, length us, event | category | flops | bytes accessed | tf_op | source)
XLA Modules:
  0.0 436.8 jit_solution(17486755455761690828)
XLA Ops:
  6.5 0.0 copy-start
  6.5 0.0 all-gather.3.cloned.1.call-start
  6.5 0.7 all-gather.3.cloned.1.call-update
  7.3 0.0 all-gather.5.cloned.1.call-start
  7.3 0.7 all-gather.5.cloned.1.call-update
  8.0 0.0 reduce-scatter.4.cloned.1.call-start
  8.1 0.9 reshape_squeeze.9
  9.0 1.3 fusion.38
  10.3 0.8 select_reduce_fusion
  11.1 0.7 compare_and_fusion
  11.8 161.0 %all-gather.3.cloned.1.call-done = bf16[1,5120,768]{2,1,0:T(8,128)(2,1)} async-done(((bf16[1,40,768]{2,1,0:T(8,128)(2,1)}), bf16[1,5120,768]{2,1,0:T(8,128)(2,1)}) %all-gather.3.cloned.1.call-update) | async-done | bytes 7864336 | tf_op jit(solution)/shard_map/all_gather | solution.py:70
  172.9 10.7 %copy.23 = bf16[1,5120,768]{1,2,0:T(8,128)(2,1)} copy(bf16[1,5120,768]{2,1,0:T(8,128)(2,1)} %all-gather.3.cloned.1.call-done) | data formatting | bytes 15728640 | tf_op jit(solution)/shard_map/all_gather | solution.py:70
  183.6 4.8 %fusion.40 = (f32[6,40]{1,0:T(8,128)S(1)}, f32[6,40,5120]{2,1,0:T(8,128)S(1)}) fusion(bf16[5120,6,128]{0,2,1:T(8,128)(2,1)} %bitcast.28, bf16[40,6,128]{2,1,0:T(8,128)(2,1)S(1)} %reshape_squeeze.9, pred[5120]{0:T(1024)(128)(4,1)S(1)} %compare_and_fusion), kind=kOutput, calls=%fused_computation.50 | convolution fusion | flops 318258944 | bytes 12847040 | tf_op jit(solution)/shard_map/qhe,khe->hqk/dot_general | solution.py:20
  188.4 0.0 copy-start.1
  188.4 2.2 copy-done.1
  190.6 1.1 fusion.1
  191.7 135.4 %all-gather.5.cloned.1.call-done = bf16[1,5120,768]{2,1,0:T(8,128)(2,1)} async-done(((bf16[1,40,768]{2,1,0:T(8,128)(2,1)}), bf16[1,5120,768]{2,1,0:T(8,128)(2,1)}) %all-gather.5.cloned.1.call-update) | async-done | bytes 7864336 | tf_op jit(solution)/shard_map/all_gather | solution.py:71
  327.1 10.4 %copy.26 = bf16[1,5120,768]{1,2,0:T(8,128)(2,1)} copy(bf16[1,5120,768]{2,1,0:T(8,128)(2,1)} %all-gather.5.cloned.1.call-done) | data formatting | bytes 15728640 | tf_op jit(solution)/shard_map/all_gather | solution.py:71
  337.5 7.6 %fusion.17 = bf16[6,5,8,128]{3,2,1,0:T(8,128)(2,1)S(1)} fusion(bf16[5120,6,128]{0,2,1:T(8,128)(2,1)} %bitcast.27, f32[6,40,5120]{2,1,0:T(8,128)} %copy-done.1, f32[6,40]{1,0:T(8,128)S(1)} %broadcast_maximum_fusion, pred[5120]{0:T(1024)(128)(4,1)S(1)} %compare_and_fusion, f32[40,6]{0,1:T(8,128)S(1)} %bitcast.31), kind=kOutput, calls=%fused_computation.13 | convolution fusion | flops 318320640 | bytes 12848000 | tf_op jit(solution)/shard_map/hqk,khe->hqe/dot_general | solution.py:27
  345.1 0.0 copy-start.4
  345.1 0.0 copy-start.3
  345.2 0.1 stack.2
  345.3 0.0 copy-start.2
  345.3 56.6 %all_to_all.5 = bf16[32,40,768]{2,1,0:T(8,128)(2,1)S(1)} all-to-all(bf16[32,40,768]{2,1,0:T(8,128)(2,1)S(1)} %stack.2), channel_id=1, replica_groups=mesh['span'=4,'seq'=32,'head'=4] {'seq'}, dimensions={0} | all-to-all | bytes 3932160 | tf_op jit(solution)/shard_map/all_to_all | solution.py:54
  401.9 0.0 copy-done
  401.9 0.8 convolution_convert_fusion
  402.7 1.1 copy.31
  403.8 0.0 reduce-scatter.4.cloned.1.call-update
  403.8 0.0 copy-done.4
  403.8 0.6 fusion.37
  404.5 0.6 iota_compare_fusion.1
  405.1 0.0 copy-done.3
  405.1 0.1 select_reduce_fusion.2
  405.2 23.2 %reduce-scatter.4.cloned.1.call-done = bf16[320,192]{1,0:T(8,128)(2,1)} async-done(((bf16[1280,192]{1,0:T(8,128)(2,1)}), bf16[320,192]{1,0:T(8,128)(2,1)}) %reduce-scatter.4.cloned.1.call-update) | async-done | bytes 122896
  428.4 1.1 copy.32
  429.5 0.0 copy-done.2
  429.5 0.8 fusion.21
  (3 shorter events, 0.0 us)
Async XLA Ops:
  6.5 395.4 %copy-start = (bf16[768,192]{0,1:T(8,128)(2,1)S(1)}, bf16[768,192]{0,1:T(8,128)(2,1)}, u32[]{:S(2)}) copy-start(bf16[768,192]{0,1:T(8,128)(2,1)} %param.16) | copy-start | bytes 884740
  6.5 166.3 %all-gather.3.cloned.1.call-start = ((), (), s32[]{:S(2)}) async-start(), calls=%async_computation.2 | async-start | bytes 7925760 | tf_op jit(solution)/shard_map/all_gather | solution.py:70
  7.3 319.8 %all-gather.5.cloned.1.call-start = ((), (), s32[]{:S(2)}) async-start(), calls=%async_computation.3 | async-start | bytes 7925760 | tf_op jit(solution)/shard_map/all_gather | solution.py:71
  8.0 420.4 %reduce-scatter.4.cloned.1.call-start = ((), (), s32[]{:S(2)}) async-start(), calls=%async_computation.4 | async-start | bytes 819200
  188.4 2.2 copy-start.1
  345.1 58.7 %copy-start.4 = (s32[4]{0:T(128)S(1)}, s32[4]{0:T(128)}, u32[]{:S(2)}) copy-start(s32[4]{0:T(128)} %param.14) | copy-start | bytes 52
  345.1 60.0 %copy-start.3 = (f32[4,192]{1,0:T(4,128)S(1)}, f32[4,192]{1,0:T(4,128)}, u32[]{:S(2)}) copy-start(f32[4,192]{1,0:T(4,128)} %param.15) | copy-start | bytes 9220
  345.3 84.2 %copy-start.2 = (bf16[1,320,192]{1,2,0:T(8,128)(2,1)S(1)}, bf16[1,320,192]{1,2,0:T(8,128)(2,1)}, u32[]{:S(2)}) copy-start(bf16[1,320,192]{1,2,0:T(8,128)(2,1)} %param.17) | copy-start | bytes 368644
Sparse Core Ops, SparseCore 0:
  12.0 160.8 all-gather.2
  177.5 149.5 all-gather.4
  403.9 24.4 reduce-scatter.3
